TPU v7x, 768 devices: a whole 4x8x12 slice. The times are simulated.
768 devices in a mesh: island: 24 (over y_lo, z), tp: 32 (over y_hi, x, core).
Axes of the slice: x: 4, y: 8 (y_hi: 4, y_lo: 2; y = y_hi * 2 + y_lo), z: 12, core: 2. Of those that a mesh axis runs over, the one named last changes fastest.
Arguments:
- tokens: bfloat16 [24, 256, 4096], P('island', 'tp'), may hold values from -6 to 6
- cotangent: bfloat16 [24, 256, 4096], P('island', 'tp'), may hold values from -1.5 to 1.5
- gate_weight: bfloat16 [4096, 7168], P(None, 'tp'), may hold values from -0.09375 to 0.09375
- up_weight: bfloat16 [4096, 7168], P(None, 'tp'), may hold values from -0.09375 to 0.09375
- down_weight: bfloat16 [7168, 4096], P('tp'), may hold values from -0.0625 to 0.0625
- local_fragment: float32 [24, 786432], P('island', 'tp'), may hold values from -9 to 9
- global_fragment: float32 [786432], P('tp'), may hold values from -6 to 6
- outer_velocity: float32 [786432], P('tp'), may hold values from -3 to 3
Outputs:
- layer_out: bfloat16 [24, 256, 4096], P('island', 'tp')
- input_grad: bfloat16 [24, 256, 4096], P('island', 'tp')
- new_fragment: float32 [786432], P('tp')
- new_velocity: float32 [786432], P('tp')
All inputs are finite; a program needn't handle non-finite values.
Results may differ from a plain program's by a relative error of at most 0.015.
Values may be sent and summed in bfloat16 or wider, within the bound.
A program may use at most 64 MiB of HBM per device.

v0:
```python
import jax
import jax.numpy as jnp
from jax import lax
from jax.sharding import PartitionSpec as P

outer_decay = 0.9
outer_stepsize = 0.7


def split_up(x, dim, length):
    shape = x.shape
    pieces = x.reshape(*shape[:dim], length, shape[dim] // length, *shape[dim + 1 :])
    return jnp.moveaxis(pieces, dim, 0)


def sent_and_summed(x, axis, dim):
    length = lax.axis_size(axis)
    pieces = lax.all_to_all(split_up(x, dim, length), axis, 0, 0, tiled=True)
    return jnp.sum(pieces, axis=0)


def turned_gather(arrays, axis, dims):
    turned = [jnp.moveaxis(a, dim, 0) for a, dim in zip(arrays, dims)]
    widths = [t[0].size for t in turned]
    both = jnp.concatenate([t.reshape(-1, w) for t, w in zip(turned, widths)], axis=1)
    filled = lax.all_gather(both, axis, axis=0, tiled=True)
    pieces = jnp.split(filled, [sum(widths[:k]) for k in range(1, len(widths))], axis=1)
    return tuple(
        (
            jnp.moveaxis(b.reshape(-1, *t.shape[1:]), 0, dim)
            for b, t, dim in zip(pieces, turned, dims)
        )
    )


def sent_together(arrays, axis, dim, along):
    both = jnp.concatenate(arrays, axis=along)
    filled, at, outs = (lax.all_gather(both, axis, axis=dim, tiled=True), 0, [])
    for a in arrays:
        outs.append(lax.slice_in_dim(filled, at, at + a.shape[along], axis=along))
        at += a.shape[along]
    return tuple(outs)


def summed_on_arrival(x, axis, dim):
    pieces = split_up(x, dim, lax.axis_size(axis))
    arrived = lax.all_to_all(pieces, axis, split_axis=0, concat_axis=0, tiled=True)
    return arrived.astype(jnp.float32).sum(axis=0)


def outer_update(local_fragment, global_fragment, outer_velocity):
    islands = lax.axis_size("island")
    difference = global_fragment - local_fragment[0]
    share_length = difference.shape[0] // islands
    offset = lax.axis_index("island") * share_length
    average = sent_and_summed(difference, "island", 0) / islands
    global_share = lax.dynamic_slice_in_dim(global_fragment, offset, share_length, 0)
    velocity_share = lax.dynamic_slice_in_dim(outer_velocity, offset, share_length, 0)
    velocity_share = outer_decay * velocity_share + average
    fragment_share = global_share - outer_stepsize * (average + outer_decay * velocity_share)
    new_fragment, new_velocity = turned_gather((fragment_share, velocity_share), "island", (0, 0))
    return (new_fragment, new_velocity)


def island_layer(tokens, cotangent, gate_weight, up_weight, down_weight):
    gathered, cotangent_all = sent_together((tokens[0], cotangent[0]), "tp", 0, 1)
    gate_value = jnp.dot(gathered, gate_weight, preferred_element_type=jnp.float32)
    up_value = jnp.dot(gathered, up_weight, preferred_element_type=jnp.float32)
    sigmoid_gate = jax.nn.sigmoid(gate_value)
    hidden = (gate_value * sigmoid_gate * up_value).astype(jnp.bfloat16)
    partial_out = jnp.dot(hidden, down_weight, preferred_element_type=jnp.float32)
    layer_out = lax.psum_scatter(
        partial_out.astype(jnp.bfloat16), "tp", scatter_dimension=0, tiled=True
    )
    hidden_grad = lax.dot_general(
        cotangent_all, down_weight, (((1,), (1,)), ((), ())), preferred_element_type=jnp.float32
    )
    up_grad = (hidden_grad * gate_value * sigmoid_gate).astype(jnp.bfloat16)
    gate_grad = (
        hidden_grad * up_value * sigmoid_gate * (1.0 + gate_value * (1.0 - sigmoid_gate))
    ).astype(jnp.bfloat16)
    first_term = lax.dot_general(
        gate_grad, gate_weight, (((1,), (1,)), ((), ())), preferred_element_type=jnp.float32
    )
    second_term = lax.dot_general(
        up_grad, up_weight, (((1,), (1,)), ((), ())), preferred_element_type=jnp.float32
    )
    partial_back = first_term + second_term
    input_grad = summed_on_arrival(partial_back.astype(jnp.bfloat16), "tp", 0)
    return (layer_out[None], input_grad.astype(jnp.bfloat16)[None])


def local(
    tokens,
    cotangent,
    gate_weight,
    up_weight,
    down_weight,
    local_fragment,
    global_fragment,
    outer_velocity,
):
    layer_out, input_grad = island_layer(tokens, cotangent, gate_weight, up_weight, down_weight)
    new_fragment, new_velocity = outer_update(local_fragment, global_fragment, outer_velocity)
    return (layer_out, input_grad, new_fragment, new_velocity)


def solution(mesh):
    in_specs = (
        P("island", "tp", None),
        P("island", "tp", None),
        P(None, "tp"),
        P(None, "tp"),
        P("tp", None),
        P("island", "tp"),
        P("tp"),
        P("tp"),
    )
    out_specs = (P("island", "tp", None), P("island", "tp", None), P("tp"), P("tp"))
    return jax.shard_map(local, mesh=mesh, in_specs=in_specs, out_specs=out_specs, check_vma=False)
```

profile of v0, /device:TPU:2, one launch (start us, length us, event | category | flops | bytes accessed | tf_op | source)
XLA Modules:
  0.0 209.4 jit_solution(14321400088673185393)
XLA Ops:
  7.2 0.0 copy-start
  7.2 0.0 all-gather.2.cloned.1.call-start
  7.2 1.6 pad_maximum_fusion
  8.9 0.0 all-gather.2.cloned.1.call-update
  8.9 1.6 sub.10
  10.5 16.4 %all-to-all-start.1 = ((f32[24,1,1024]{2,1,0:T(1,128)}), f32[24,1,1024]{2,1,0:T(1,128)S(1)}, u32[]{:S(2)}, u32[]{:S(2)}) async-start(f32[24,1,1024]{2,1,0:T(1,128)} %bitcast.6), calls=%async_computation.2 | async-start | bytes 196608 | tf_op jit(solution)/shard_map/all_to_all | solution.py:18
  26.9 0.0 reduce-scatter.2.cloned.1.call-start
  26.9 11.7 %all-to-all-done.1 = f32[24,1,1024]{2,1,0:T(1,128)S(1)} async-done(((f32[24,1,1024]{2,1,0:T(1,128)}), f32[24,1,1024]{2,1,0:T(1,128)S(1)}, u32[]{:S(2)}, u32[]{:S(2)}) %all-to-all-start.1) | async-done | bytes 98336 | tf_op jit(solution)/shard_map/all_to_all | solution.py:18
  38.7 0.1 reduce_sum.22
  38.7 0.7 multiply_subtract_fusion
  39.5 46.2 %all_gather.7 = f32[24576,2]{0,1:T(2,128)S(1)} all-gather(f32[1024,2]{0,1:T(2,128)S(1)} %pad_maximum_fusion.1), channel_id=1, replica_groups=mesh['island'=24,'tp'=32] {'island'}, dimensions={0}, use_global_device_ids=true | all-gather | bytes 204800 | tf_op jit(solution)/shard_map/all_gather | solution.py:26
  85.7 4.5 %all-gather.2.cloned.1.call-done = bf16[256,8192]{1,0:T(8,128)(2,1)} async-done(((bf16[8,8192]{1,0:T(8,128)(2,1)}), bf16[256,8192]{1,0:T(8,128)(2,1)}) %all-gather.2.cloned.1.call-update) | async-done | bytes 4194320 | tf_op jit(solution)/shard_map/all_gather | solution.py:38
  90.2 0.0 copy-start.1
  90.2 3.1 %fusion.4 = f32[256,224]{0,1:T(8,128)S(1)} fusion(bf16[4096,224]{0,1:T(8,128)(2,1)} %param.11, bf16[256,8192]{1,0:T(8,128)(2,1)} %all-gather.2.cloned.1.call-done), kind=kOutput, calls=%fused_computation.6 | convolution fusion | flops 469762048 | bytes 4161536 | tf_op jit(solution)/shard_map/dot_general | solution.py:68
  93.3 0.0 copy-done.1
  93.3 2.4 %fusion.6 = f32[256,224]{0,1:T(8,128)S(1)} fusion(bf16[4096,224]{0,1:T(8,128)(2,1)S(1)} %copy-done.1, bf16[256,8192]{1,0:T(8,128)(2,1)} %all-gather.2.cloned.1.call-done), kind=kOutput, calls=%fused_computation.8 | convolution fusion | flops 469762048 | bytes 4161536 | tf_op jit(solution)/shard_map/dot_general | solution.py:67
  95.7 0.0 copy-done
  95.7 2.1 convolution_convert_fusion
  97.8 0.0 reduce-scatter.2.cloned.1.call-update
  97.8 0.0 copy-start.2
  97.8 2.5 %fusion.2 = f32[256,224]{0,1:T(8,128)S(1)} fusion(bf16[224,4096]{1,0:T(8,128)(2,1)S(1)} %copy-done, bf16[256,8192]{1,0:T(8,128)(2,1)} %all-gather.2.cloned.1.call-done), kind=kOutput, calls=%fused_computation.4 | convolution fusion | flops 469762048 | bytes 4161536 | tf_op jit(solution)/shard_map/dot_general | solution.py:75
  100.3 0.0 copy-done.2
  100.3 0.0 copy-start.3
  100.3 0.8 fusion.8
  101.1 0.7 copy-done.3
  101.8 2.1 fusion.1
  103.9 6.8 %all-to-all-start = ((bf16[32,8,4096]{2,1,0:T(8,128)(2,1)}), bf16[32,8,4096]{2,1,0:T(8,128)(2,1)}, u32[]{:S(2)}, u32[]{:S(2)}) async-start(bf16[32,8,4096]{2,1,0:T(8,128)(2,1)} %fusion.1), calls=%async_computation.1 | async-start | bytes 4194304 | tf_op jit(solution)/shard_map/all_to_all | solution.py:47
  110.7 0.8 fusion.15
  111.5 48.8 %all-to-all-done = bf16[32,8,4096]{2,1,0:T(8,128)(2,1)} async-done(((bf16[32,8,4096]{2,1,0:T(8,128)(2,1)}), bf16[32,8,4096]{2,1,0:T(8,128)(2,1)}, u32[]{:S(2)}, u32[]{:S(2)}) %all-to-all-start) | async-done | bytes 2097184 | tf_op jit(solution)/shard_map/all_to_all | solution.py:47
  160.3 2.5 %reduce_sum.21 = bf16[8,4096]{1,0:T(8,128)(2,1)} reduce(bf16[32,8,4096]{2,1,0:T(8,128)(2,1)} %all-to-all-done, bf16[]{:T(256)} %constant.4.clone.1), dimensions={0}, to_apply=%region_1.0 | reduce | flops 1015808 | bytes 2162690 | tf_op jit(solution)/shard_map/reduce_sum | solution.py:48
  162.8 39.8 %reduce-scatter.2.cloned.1.call-done = bf16[8,4096]{1,0:T(8,128)(2,1)} async-done(((bf16[256,4096]{1,0:T(8,128)(2,1)}), bf16[8,4096]{1,0:T(8,128)(2,1)}) %reduce-scatter.2.cloned.1.call-update) | async-done | bytes 65552 | tf_op jit(solution)/shard_map/reduce_scatter | solution.py:72
  (1 shorter events, 0.0 us)
Async XLA Ops:
  7.2 88.5 %copy-start = (bf16[224,4096]{1,0:T(8,128)(2,1)S(1)}, bf16[224,4096]{1,0:T(8,128)(2,1)}, u32[]{:S(2)}) copy-start(bf16[224,4096]{1,0:T(8,128)(2,1)} %param.12) | copy-start | bytes 5505028
  7.2 83.0 %all-gather.2.cloned.1.call-start = ((), (), s32[]{:S(2)}) async-start(), calls=%async_computation.3 | async-start | bytes 4325376 | tf_op jit(solution)/shard_map/all_gather | solution.py:38
  10.5 28.2 %all-to-all-start.1 = ((f32[24,1,1024]{2,1,0:T(1,128)}), f32[24,1,1024]{2,1,0:T(1,128)S(1)}, u32[]{:S(2)}, u32[]{:S(2)}) async-start(f32[24,1,1024]{2,1,0:T(1,128)} %bitcast.6), calls=%async_computation.2 | async-start | bytes 196608 | tf_op jit(solution)/shard_map/all_to_all | solution.py:18
  26.9 175.7 %reduce-scatter.2.cloned.1.call-start = ((), (), s32[]{:S(2)}) async-start(), calls=%async_computation.4 | async-start | bytes 2162688 | tf_op jit(solution)/shard_map/reduce_scatter | solution.py:72
  90.2 3.1 %copy-start.1 = (bf16[4096,224]{0,1:T(8,128)(2,1)S(1)}, bf16[4096,224]{0,1:T(8,128)(2,1)}, u32[]{:S(2)}) copy-start(bf16[4096,224]{0,1:T(8,128)(2,1)} %param.10) | copy-start | bytes 5505028
  97.8 2.5 %copy-start.2 = (bf16[4096,224]{0,1:T(8,128)(2,1)S(1)}, bf16[4096,224]{0,1:T(8,128)(2,1)}, u32[]{:S(2)}) copy-start(bf16[4096,224]{0,1:T(8,128)(2,1)} %param.10) | copy-start | bytes 5505028
  100.3 1.5 copy-start.3
  103.9 56.4 %all-to-all-start = ((bf16[32,8,4096]{2,1,0:T(8,128)(2,1)}), bf16[32,8,4096]{2,1,0:T(8,128)(2,1)}, u32[]{:S(2)}, u32[]{:S(2)}) async-start(bf16[32,8,4096]{2,1,0:T(8,128)(2,1)} %fusion.1), calls=%async_computation.1 | async-start | bytes 4194304 | tf_op jit(solution)/shard_map/all_to_all | solution.py:47
Sparse Core Ops, SparseCore 0:
  11.7 78.4 all-gather.1
  97.9 104.6 reduce-scatter.1
where the time goes:
time: 210 us; the launch traced here: 209 us
  waiting for transfers between devices  105 us (50%)
  blocking collectives  46.2 us (22%)
  starting transfers between devices  23.2 us (11%)
  between operations  14.1 us (7%)
  matrix products  12.9 us (6%)
  other arithmetic  6.56 us (3%)
    all_to_all x1, waiting for transfers between devices, summed_on_arrival(): lax.all_to_all(pieces, axis, split_axis=0, concat_axis=0, tiled=True)  48.8 us
    all_gather x1, blocking collectives, turned_gather(): filled = lax.all_gather(both, axis, axis=0, tiled=True)  46.2 us
    reduce_scatter x1, waiting for transfers between devices, island_layer(): lax.psum_scatter(partial_out.astype(jnp.bfloat16), 'tp', scatter_dimensio...  39.8 us
    all_to_all x1, starting transfers between devices, sent_and_summed(): pieces = lax.all_to_all(split_up(x, dim, length), axis, 0, 0, tiled=True)  16.4 us
    all_to_all x1, waiting for transfers between devices, sent_and_summed(): pieces = lax.all_to_all(split_up(x, dim, length), axis, 0, 0, tiled=True)  11.7 us
    all_to_all x1, starting transfers between devices, summed_on_arrival(): lax.all_to_all(pieces, axis, split_axis=0, concat_axis=0, tiled=True)  6.78 us
    all_gather x1, waiting for transfers between devices, sent_together(): filled, at, outs = (lax.all_gather(both, axis, axis=dim, tiled=True), 0, [])  4.53 us
  transfers between devices with their start and end apart: 4, of which 4 were waited for; matrix products, arithmetic and copies ran while one was open for 5% of the time, Pallas kernels for 0%

commit v1 on v0

v1 whole, which is shorter than its diff:
```python
import jax
import jax.numpy as jnp
from jax import lax
from jax.experimental import pallas as pl
from jax.experimental.pallas import tpu as pltpu
from jax.sharding import PartitionSpec as P

outer_decay = 0.9
outer_stepsize = 0.7

MESH = pl.DeviceIdType.MESH
BF, F32 = jnp.bfloat16, jnp.float32
NX, NYH, NYL, NZ = 4, 4, 2, 12
ISLANDS = NYL * NZ
ROWS, D, WIDTH = 8, 4096, 224
FRAG_ROWS = 192
ZROWS = FRAG_ROWS // NZ
TILE = 512

DYS = (-1, 1, 2, 0)
DXS = (0, -1, 1, 2)


def slot(dy, dx):
    return pl.ds((DYS.index(dy) * 4 + DXS.index(dx)) * ROWS, ROWS)


def nt(a, b):
    return lax.dot_general(a, b, (((1,), (1,)), ((), ())), preferred_element_type=F32)


def nn(a, b):
    return jnp.dot(a, b, preferred_element_type=F32)


def kernel(
    tok, cot, wg, wu, wd, lfrag, gfrag, vel,
    o_layer, o_grad, o_frag, o_vel,
    xc, w, pb, hid, gg, ug, rf, rd, sy, ry, r0, ob,
    fl, fg, fv, rz, s12, sp, av, nf, nv,
    lsem, ssem, rsem, ysem, zsem, zsem2,
):
    island, tp = lax.axis_index("island"), lax.axis_index("tp")
    core, x, yh = lax.rem(tp, 2), lax.rem(tp // 2, NX), tp // (2 * NX)
    yl, z = island // NZ, lax.rem(island, NZ)

    def at(dx=0, dy=0, dz=0, dyl=0, dc=0):
        zz, yy = lax.rem(z + dz + NZ, NZ), lax.rem(yh + dy + NYH, NYH)
        xx = lax.rem(x + dx + NX, NX)
        return (lax.rem(yl + dyl, NYL) * NZ + zz, (yy * NX + xx) * 2 + lax.rem(core + dc, 2))

    copies = {}

    def send(name, src, dst, to):
        k = len(copies)
        copies[name] = pltpu.make_async_remote_copy(
            src_ref=src, dst_ref=dst, send_sem=ssem.at[k], recv_sem=rsem.at[k],
            device_id=to, device_id_type=MESH,
        )
        copies[name].start()

    def recv(*name):
        copies[name].wait_recv()

    def signal(sem, to):
        pl.semaphore_signal(sem, inc=1, device_id=to, device_id_type=MESH)

    loads = []

    def load(src, dst):
        cp = pltpu.make_async_copy(src, dst, lsem.at[len(loads)])
        cp.start()
        loads.append(cp)
        return cp

    barrier = pltpu.get_barrier_semaphore()
    near = [dict(dx=1), dict(dx=-1), dict(dy=1), dict(dy=-1), dict(dc=1), dict(dyl=1)]
    near += [dict(dz=1), dict(dz=-1), dict(dz=2), dict(dz=-2)]
    for k in near:
        signal(barrier, at(**k))
    own = [load(tok.at[0], xc.at[0, slot(0, 0)]), load(cot.at[0], xc.at[1, slot(0, 0)])]
    frag_loads = [load(lfrag, fl), load(gfrag, fg), load(vel, fv)]
    weights = [load(wt, w.at[i, pl.ds(0, WIDTH)]) for i, wt in enumerate((wg, wu, wd))]
    pl.semaphore_wait(barrier, len(near))

    for i, src in ((0, tok), (1, cot)):
        for s in (1, -1):
            send(("x", 0, s, i), src.at[0], xc.at[i, slot(0, -s)], at(dx=s))
        for s in (1, -1):
            send(("y", s, i), src.at[0], xc.at[i, slot(-s, 0)], at(dy=s))
    for s in (1, -1):
        signal(ysem, at(dy=s))
        signal(zsem, at(dz=2 * s))
    for i, wt in enumerate((wg, wu, wd)):
        send(("w", i), wt, w.at[i, pl.ds(WIDTH, WIDTH)], at(dc=1))
    pl.semaphore_wait(ysem, 2)
    for i, src in ((0, tok), (1, cot)):
        send(("y", 2, i), src.at[0], xc.at[i, slot(2, 0)], at(dy=2))
    pl.semaphore_wait(zsem, 2)
    for s in (1, -1):
        signal(zsem2, at(dz=2 * s))

    def spread(dy, i):
        recv("y", 2 if dy == 2 else -dy, i)
        for s in (1, -1):
            send(("x", dy, s, i), xc.at[i, slot(dy, 0)], xc.at[i, slot(dy, -s)], at(dx=s))

    def relay(dy):
        recv("x", dy, 1, 0)
        send(("f", dy, 0), xc.at[0, slot(dy, -1)], xc.at[0, slot(dy, 2)], at(dx=1))
        recv("x", dy, -1, 1)
        send(("f", dy, 1), xc.at[1, slot(dy, 1)], xc.at[1, slot(dy, 2)], at(dx=-1))

    def arrived(dy):
        recv("x", dy, -1, 0)
        recv("x", dy, 1, 1)
        recv("f", dy, 0)
        recv("f", dy, 1)

    for cp in frag_loads:
        cp.wait()
    fl[...] = fg[...] - fl[...]
    pl.semaphore_wait(zsem2, 2)
    for k in range(1, NZ):
        there = lax.rem(z + k, NZ)
        part = pl.ds(pl.multiple_of(there * ZROWS, ZROWS), ZROWS)
        send(("z", k), fl.at[part], rz.at[k - 1], at(dz=k))
    mine = pl.ds(pl.multiple_of(z * ZROWS, ZROWS), ZROWS)

    def outer_sum():
        total = fl[mine, :]
        for k in range(1, NZ):
            recv("z", k)
            total = total + rz[k - 1]
        s12[...] = total
        send(("p",), s12, sp, at(dyl=1))

    def outer_spread():
        recv("p")
        av[mine, :] = (s12[...] + sp[...]) / ISLANDS
        for k in range(1, NZ):
            send(("a", k), av.at[mine], av.at[mine], at(dz=k))

    def outer_update():
        for k in range(1, NZ):
            recv("a", k)
        average = av[...]
        velocity = outer_decay * fv[...] + average
        nv[...] = velocity
        nf[...] = fg[...] - outer_stepsize * (average + outer_decay * velocity)
        return [load(nf, o_frag), load(nv, o_vel)]

    for cp in own:
        cp.wait()
    relay(0)
    for i in (0, 1):
        for dy in (-1, 1):
            spread(dy, i)
    for dy in (-1, 1):
        relay(dy)
    spread(2, 0)
    for cp in weights:
        cp.wait()
    for i in range(3):
        recv("w", i)
    for dy in (-1, 1):
        arrived(dy)

    def gradients(rows, between):
        tokens, cotangent = xc[0, rows, :], xc[1, rows, :]
        gate = nt(tokens, w[0])
        between[0]()
        up = nt(tokens, w[1])
        between[1]()
        grad = nt(cotangent, w[2])
        s = jax.nn.sigmoid(gate)
        hid[...] = (gate * s * up).astype(BF)
        ug[...] = (grad * gate * s).astype(BF)
        gg[...] = (grad * up * s * (1.0 + gate * (1.0 - s))).astype(BF)
        between[2]()

    def tiles(fill):
        @pl.loop(0, D // TILE)
        def _(t):
            fill(pl.ds(pl.multiple_of(t * TILE, TILE), TILE))

    def layer_part(rows):
        def fill(cols):
            pb[0, rows, cols] = nn(hid[...], w[2, :, cols]).astype(BF)

        tiles(fill)

    def grad_part(rows):
        def fill(cols):
            both = nn(gg[...], w[0, :, cols]) + nn(ug[...], w[1, :, cols])
            pb[1, rows, cols] = both.astype(BF)

        tiles(fill)

    def scatter(dys, i):
        ahead = 1 if i == 0 else -1
        for dy in dys:
            k = DYS.index(dy)
            send(("rf", dy, i), pb.at[i, slot(dy, 2)], rf.at[i, k], at(dx=ahead))
            send(("rd", dy, -ahead, i), pb.at[i, slot(dy, -ahead)], rd.at[0, i, k], at(dx=-ahead))

    def add_on(dy, i):
        ahead = 1 if i == 0 else -1
        k = DYS.index(dy)
        recv("rf", dy, i)
        here = slot(dy, ahead)
        pb[i, here, :] = (pb[i, here, :].astype(F32) + rf[i, k].astype(F32)).astype(BF)
        send(("rd", dy, ahead, i), pb.at[i, here], rd.at[1, i, k], at(dx=ahead))

    def line_sum(dy, i):
        k = DYS.index(dy)
        recv("rd", dy, 1, i)
        recv("rd", dy, -1, i)
        total = pb[i, slot(dy, 0), :].astype(F32) + rd[0, i, k].astype(F32)
        total = total + rd[1, i, k].astype(F32)
        if dy == 0:
            r0[i] = total
        else:
            sy[k, i] = total.astype(BF)
            send(("ry", dy, i), sy.at[k, i], ry.at[k, i], at(dy=dy))

    first, second = pl.ds(0, 64), pl.ds(64, 64)

    def nothing():
        pass

    def step_c2():
        spread(2, 1)

    gradients(first, (step_c2, lambda: relay(2), outer_sum))
    layer_part(first)
    scatter((-1, 1), 0)
    grad_part(first)
    scatter((-1, 1), 1)
    outer_spread()
    arrived(0)
    arrived(2)

    def adds():
        for dy in (-1, 1):
            add_on(dy, 0)
            add_on(dy, 1)

    def lines():
        for dy in (-1, 1):
            for i in (0, 1):
                line_sum(dy, i)

    gradients(second, (nothing, adds, nothing))
    layer_part(second)
    scatter((2, 0), 0)
    grad_part(second)
    scatter((2, 0), 1)
    lines()
    stores = outer_update()
    for dy in (2, 0):
        add_on(dy, 0)
        add_on(dy, 1)
    for dy in (2, 0):
        for i in (0, 1):
            line_sum(dy, i)
    for i, out in ((0, o_layer), (1, o_grad)):
        total = r0[i]
        for dy in (-1, 1, 2):
            recv("ry", dy, i)
            total = total + ry[DYS.index(dy), i].astype(F32)
        ob[i] = total.astype(BF)
        stores.append(load(ob.at[i], out.at[0]))
    for cp in copies.values():
        cp.wait_send()
    for cp in stores:
        cp.wait()


def step(tokens, cotangent, gate_weight, up_weight, down_weight, local_fragment, global_fragment, outer_velocity):
    frag = jax.ShapeDtypeStruct((FRAG_ROWS, 128), F32)
    rows = jax.ShapeDtypeStruct((1, ROWS, D), BF)
    sends = 120
    vm = pltpu.VMEM
    layer_out, input_grad, new_fragment, new_velocity = pl.pallas_call(
        kernel,
        out_shape=(rows, rows, frag, frag),
        in_specs=[pl.BlockSpec(memory_space=pl.ANY)] * 8,
        out_specs=[pl.BlockSpec(memory_space=pl.ANY)] * 4,
        scratch_shapes=[
            vm((2, 128, D), BF),
            vm((3, 2 * WIDTH, D), BF),
            vm((2, 128, D), BF),
            vm((64, 2 * WIDTH), BF),
            vm((64, 2 * WIDTH), BF),
            vm((64, 2 * WIDTH), BF),
            vm((2, 4, ROWS, D), BF),
            vm((2, 2, 4, ROWS, D), BF),
            vm((3, 2, ROWS, D), BF),
            vm((3, 2, ROWS, D), BF),
            vm((2, ROWS, D), F32),
            vm((2, ROWS, D), BF),
            vm((FRAG_ROWS, 128), F32),
            vm((FRAG_ROWS, 128), F32),
            vm((FRAG_ROWS, 128), F32),
            vm((NZ - 1, ZROWS, 128), F32),
            vm((ZROWS, 128), F32),
            vm((ZROWS, 128), F32),
            vm((FRAG_ROWS, 128), F32),
            vm((FRAG_ROWS, 128), F32),
            vm((FRAG_ROWS, 128), F32),
            pltpu.SemaphoreType.DMA((16,)),
            pltpu.SemaphoreType.DMA((sends,)),
            pltpu.SemaphoreType.DMA((sends,)),
            pltpu.SemaphoreType.REGULAR,
            pltpu.SemaphoreType.REGULAR,
            pltpu.SemaphoreType.REGULAR,
        ],
        compiler_params=pltpu.CompilerParams(
            collective_id=0, has_side_effects=True, vmem_limit_bytes=67043328
        ),
        name="diloco_step",
    )(
        tokens,
        cotangent,
        gate_weight.T,
        up_weight.T,
        down_weight,
        local_fragment.reshape(FRAG_ROWS, 128),
        global_fragment.reshape(FRAG_ROWS, 128),
        outer_velocity.reshape(FRAG_ROWS, 128),
    )
    return layer_out, input_grad, new_fragment.reshape(-1), new_velocity.reshape(-1)


def solution(mesh):
    in_specs = (
        P("island", "tp", None),
        P("island", "tp", None),
        P(None, "tp"),
        P(None, "tp"),
        P("tp", None),
        P("island", "tp"),
        P("tp"),
        P("tp"),
    )
    out_specs = (P("island", "tp", None), P("island", "tp", None), P("tp"), P("tp"))
    return jax.shard_map(step, mesh=mesh, in_specs=in_specs, out_specs=out_specs, check_vma=False)
```

time: 210 us -> 80.3 us (0.38)
  the two profiles are of different devices: /device:TPU:2 before, /device:TPU:8 now
where the time goes in v1:
time: 80.3 us; the launch traced here: 80 us
  Pallas kernels  73.4 us (91%)
  local copies, waits for them, and re-layouts  6.02 us (7%)
    pallas_call x1, Pallas kernels, step(): pl.pallas_call(kernel, out_shape=(rows, rows, frag, frag), in_specs=[pl.B...  73.4 us
    unnamed x4, local copies, waits for them, and re-layouts  6.02 us

profile of v1, /device:TPU:8, one launch (start us, length us, event | category | flops | bytes accessed | tf_op | source)
XLA Modules:
  0.0 80.0 jit_solution(16486769292666780426)
XLA Ops:
  0.6 73.4 %diloco_step.1 = (bf16[1,8,4096]{2,1,0:T(8,128)(2,1)}, bf16[1,8,4096]{2,1,0:T(8,128)(2,1)}, f32[192,128]{1,0:T(8,128)}, f32[192,128]{1,0:T(8,128)}) custom-call(bf16[1,8,4096]{2,1,0:T(8,128)(2,1)} %tok.1, bf16[1,8,4096]{2,1,0:T(8,128)(2,1)} %cot.1, bf16[224,4096]{1,0:T(8,128)(2,1)} %bitcast.7, bf16[224,4096]{1,0:T(8,128)(2,1)} %bitcast.8, ...), custom_call_target="tpu_custom_call" | custom-call | tf_op jit(solution)/shard_map/diloco_step/pallas_call | solution.py:285
  74.0 1.5 %copy.16 = bf16[1,8,4096]{2,1,0:T(8,128)(2,1)} copy(bf16[1,8,4096]{2,1,0:T(8,128)(2,1)} %get-tuple-element.16) | data formatting | bytes 131072
  75.5 1.5 %copy.17 = bf16[1,8,4096]{2,1,0:T(8,128)(2,1)} copy(bf16[1,8,4096]{2,1,0:T(8,128)(2,1)} %get-tuple-element.17) | data formatting | bytes 131072
  77.0 1.5 %copy.18 = f32[24576]{0:T(1024)} copy(f32[24576]{0:T(1024)} %bitcast.10) | data formatting | bytes 196608
  78.5 1.5 %copy.19 = f32[24576]{0:T(1024)} copy(f32[24576]{0:T(1024)} %bitcast.9) | data formatting | bytes 196608
